TPU v7x, 32 devices: a whole 2x2x4 slice. The times are simulated.
32 devices in a mesh: sect: 2 (over core), tok: 2 (over x), vocab: 8 (over z, y).
Axes of the slice: x: 2, y: 2, z: 4, core: 2. Of those that a mesh axis runs over, the one named last changes fastest.
Arguments:
- teacher_hidden: bfloat16 [512, 8192], P('tok', 'sect'), may hold values from -6 to 6
- teacher_head: bfloat16 [8192, 4096], P('sect', 'vocab'), may hold values from -0.19921875 to 0.19921875
- student_hidden: bfloat16 [512, 3072], P('tok', 'sect'), may hold values from -6 to 6
- student_head: bfloat16 [3072, 4096], P('sect', 'vocab'), may hold values from -0.328125 to 0.328125
- live_counts: int32 [2], P('tok'), may hold values from 1 to 256, 384 in all
Outputs:
- loss: float32 [], replicated
- head_grad: bfloat16 [3072, 4096], P(('sect', 'tok'), 'vocab')
- hidden_grad: bfloat16 [512, 3072], P(('tok', 'vocab'), 'sect')
Inputs may be any that keep to these rules, and one draw needn't show every extreme that they name: Shard k of the tokens has its first live_counts[k] token slots live and the rest empty.
All inputs are finite; a program needn't handle non-finite values.
Results may differ from a plain program's by a relative error of at most 0.0049.
Values may be sent and summed in bfloat16 or wider, within the bound.
A program may use at most 64 MiB of HBM per device.

v0:
```python
import jax
import jax.numpy as jnp
from jax import lax
from jax.sharding import PartitionSpec as P


def softened(teacher_logits, student_logits):
    teacher = teacher_logits * 0.5
    student = student_logits * 0.5
    teacher_exp = jnp.exp(teacher)
    student_exp = jnp.exp(student)
    partial_sums = (
        jnp.sum(teacher_exp, axis=1),
        jnp.sum(student_exp, axis=1),
        jnp.sum(teacher_exp * (teacher - student), axis=1),
    )
    return (teacher_exp, student_exp, partial_sums)


def finish(teacher_exp, student_exp, totals, live_rows, live_total, vocab_entries):
    teacher_sum, student_sum, cross = totals
    divergence = cross / teacher_sum - jnp.log(teacher_sum) + jnp.log(student_sum)
    numerator = jnp.sum(live_rows * divergence)
    row_scale = live_rows * (32.0 * vocab_entries * 0.5 / live_total)
    logit_grad = (
        row_scale[:, None]
        * (student_exp / student_sum[:, None] - teacher_exp / teacher_sum[:, None])
    ).astype(jnp.bfloat16)
    return (logit_grad, numerator)


def body(teacher_hidden, teacher_head, student_hidden, student_head, live_counts):
    token_rows = teacher_hidden.shape[0]
    vocab_entries = student_head.shape[1] * lax.axis_size("vocab")
    live_total = lax.psum(jnp.sum(live_counts.astype(jnp.float32)), "tok")
    live_rows = (jnp.arange(token_rows, dtype=jnp.int32) < live_counts[0]).astype(jnp.float32)
    teacher_part = jnp.dot(teacher_hidden, teacher_head, preferred_element_type=jnp.float32)
    student_part = jnp.dot(student_hidden, student_head, preferred_element_type=jnp.float32)
    teacher_logits, student_logits = lax.psum((teacher_part, student_part), "sect")
    teacher_exp, student_exp, partial_sums = softened(teacher_logits, student_logits)
    totals = lax.psum((partial_sums[0], partial_sums[1], partial_sums[2]), "vocab")
    logit_grad, numerator = finish(
        teacher_exp, student_exp, totals, live_rows, live_total, vocab_entries
    )
    owned_features = lax.all_to_all(student_hidden, "tok", split_axis=1, concat_axis=0, tiled=True)
    head_sum = lax.dot_general(
        owned_features,
        lax.all_gather(logit_grad, "tok", axis=0, tiled=True),
        (((0,), (0,)), ((), ())),
        preferred_element_type=jnp.float32,
    )
    head_grad = head_sum.astype(jnp.bfloat16)
    hidden_grad = lax.psum_scatter(
        lax.dot_general(
            logit_grad, student_head, (((1,), (1,)), ((), ())), preferred_element_type=jnp.float32
        ),
        "vocab",
        scatter_dimension=0,
        tiled=True,
    ).astype(jnp.bfloat16)
    loss = lax.psum(numerator, "tok") / live_total
    return (loss, head_grad, hidden_grad)


def solution(mesh):
    placed = (P("tok", "sect"), P("sect", "vocab"), P("tok", "sect"), P("sect", "vocab"), P("tok"))
    return jax.shard_map(
        body,
        mesh=mesh,
        in_specs=placed,
        out_specs=(P(), P(("sect", "tok"), "vocab"), P(("tok", "vocab"), "sect")),
        check_vma=False,
    )
```

profile of v0, /device:TPU:0, one launch (start us, length us, event | category | flops | bytes accessed | tf_op | source)
XLA Modules:
  0.0 144.1 jit_solution(9674600153131628786)
XLA Ops:
  7.2 0.0 copy-start
  7.2 0.0 copy-start.2
  7.2 0.0 all-reduce.5.cloned.1.call-start
  7.2 1.5 %copy-done = bf16[256,4096]{1,0:T(8,128)(2,1)S(1)} copy-done((bf16[256,4096]{1,0:T(8,128)(2,1)S(1)}, bf16[256,4096]{1,0:T(8,128)(2,1)}, u32[]{:S(2)}) %copy-start) | copy-done | bytes 2097176
  8.8 4.3 %fusion.3 = f32[256,512]{1,0:T(8,128)} fusion(bf16[256,4096]{1,0:T(8,128)(2,1)S(1)} %copy-done, bf16[4096,512]{1,0:T(8,128)(2,1)} %param.6), kind=kOutput, calls=%fused_computation.10 | convolution fusion | flops 1073741824 | bytes 6815744 | tf_op jit(solution)/shard_map/dot_general | solution.py:37
  13.1 1.4 fusion.4
  14.5 0.0 all-reduce.5.cloned.1.call-update
  14.5 0.0 reduce-scatter.2.cloned.1.call-start
  15.2 21.8 %all-reduce.5.cloned.1.call-done = (f32[256,512]{1,0:T(8,128)}, f32[256,512]{1,0:T(8,128)}) async-done(((f32[256,512]{1,0:T(8,128)}, f32[256,512]{1,0:T(8,128)}), (f32[256,512]{1,0:T(8,128)}, f32[256,512]{1,0:T(8,128)})) %all-reduce.5.cloned.1.call-update) | async-done | bytes 1048592 | tf_op jit(solution)/shard_map/psum | solution.py:39
  37.0 1.5 %multiply_reduce_fusion = (f32[256]{0:T(256)S(1)}, f32[256]{0:T(256)S(1)}, f32[256]{0:T(256)S(1)}) fusion(f32[256,512]{1,0:T(8,128)} %get-tuple-element.20, f32[256,512]{1,0:T(8,128)} %get-tuple-element.21), kind=kLoop, calls=%fused_computation.3 | loop fusion | flops 916736 | bytes 1051648 | tf_op jit(solution)/shard_map/reduce_sum | solution.py:15
  38.6 21.6 %all-reduce = (f32[256]{0:T(256)S(1)}, f32[256]{0:T(256)S(1)}, f32[256]{0:T(256)S(1)}) all-reduce(f32[256]{0:T(256)S(1)} %get-tuple-element.13, f32[256]{0:T(256)S(1)} %get-tuple-element.14, f32[256]{0:T(256)S(1)} %get-tuple-element.12), channel_id=1, replica_groups=mesh['sect'=2,'tok'=2,'vocab'=8] {'vocab'}, use_global_device_ids=true, to_apply=%region_7.0 | all-reduce | flops 768 | bytes 6144 | tf_op jit(solution)/shard_map/psum | solution.py:41
  60.2 0.6 select_reduce_fusion
  60.8 6.2 %all-reduce.1 = (f32[]{:T(128)}, f32[]{:T(128)}) all-reduce(f32[]{:T(128)} %select_reduce_fusion, f32[]{:T(128)} %bitcast.1), channel_id=1, replica_groups=mesh['sect'=2,'tok'=2,'vocab'=8] {'tok'}, use_global_device_ids=true, to_apply=%region_9.0 | all-reduce | flops 2 | bytes 16 | tf_op jit(solution)/shard_map/psum | solution.py:61
  67.7 1.4 multiply_convert_fusion
  69.1 3.2 %fusion.5 = f32[256,1536]{1,0:T(8,128)} fusion(bf16[256,512]{1,0:T(8,128)(2,1)S(1)} %multiply_convert_fusion, bf16[1536,512]{1,0:T(8,128)(2,1)} %param.8), kind=kOutput, calls=%fused_computation.12 | convolution fusion | flops 402653184 | bytes 3407872 | tf_op jit(solution)/shard_map/dot_general | solution.py:54
  72.3 0.0 reduce-scatter.2.cloned.1.call-update
  72.3 1.2 copy.10
  73.4 11.5 %all_to_all.19 = bf16[256,2,768]{0,2,1:T(8,128)(2,1)S(1)} all-to-all(bf16[256,2,768]{0,2,1:T(8,128)(2,1)} %bitcast.18), channel_id=1, replica_groups=mesh['sect'=2,'tok'=2,'vocab'=8] {'tok'}, dimensions={1} | all-to-all | bytes 1572864 | tf_op jit(solution)/shard_map/all_to_all | solution.py:45
  84.9 1.2 copy.11
  87.4 7.0 %all_gather.3 = bf16[512,512]{1,0:T(8,128)(2,1)S(1)} all-gather(bf16[256,512]{1,0:T(8,128)(2,1)S(1)} %multiply_convert_fusion), channel_id=1, replica_groups=mesh['sect'=2,'tok'=2,'vocab'=8] {'tok'}, dimensions={0}, use_global_device_ids=true | all-gather | bytes 786432 | tf_op jit(solution)/shard_map/all_gather | solution.py:48
  94.5 1.7 %fusion = bf16[768,512]{0,1:T(8,128)(2,1)S(1)} fusion(bf16[512,512]{1,0:T(8,128)(2,1)S(1)} %all_gather.3, bf16[512,768]{1,0:T(8,128)(2,1)} %bitcast.19), kind=kOutput, calls=%fused_computation.1 | convolution fusion | flops 403046400 | bytes 2097152 | tf_op jit(solution)/shard_map/dot_general | solution.py:46
  96.2 1.2 copy.12
  97.4 37.2 %reduce-scatter.2.cloned.1.call-done = f32[32,1536]{1,0:T(8,128)} async-done(((f32[256,1536]{1,0:T(8,128)}), f32[32,1536]{1,0:T(8,128)}) %reduce-scatter.2.cloned.1.call-update) | async-done | bytes 196624 | tf_op jit(solution)/shard_map/reduce_scatter | solution.py:53
  134.5 1.6 %convert_element_type.20 = bf16[32,1536]{1,0:T(8,128)(2,1)} convert(f32[32,1536]{1,0:T(8,128)} %reduce-scatter.2.cloned.1.call-done) | non-fusion elementwise | flops 49152 | bytes 294912 | tf_op jit(solution)/shard_map/convert_element_type | solution.py:60
  (4 shorter events, 0.0 us)
Async XLA Ops:
  7.2 1.6 %copy-start = (bf16[256,4096]{1,0:T(8,128)(2,1)S(1)}, bf16[256,4096]{1,0:T(8,128)(2,1)}, u32[]{:S(2)}) copy-start(bf16[256,4096]{1,0:T(8,128)(2,1)} %param.5) | copy-start | bytes 6291460
  7.2 5.9 %copy-start.2 = (bf16[256,1536]{1,0:T(8,128)(2,1)S(1)}, bf16[256,1536]{1,0:T(8,128)(2,1)}, u32[]{:S(2)}) copy-start(bf16[256,1536]{1,0:T(8,128)(2,1)} %param.7) | copy-start | bytes 2359300
  7.2 29.9 %all-reduce.5.cloned.1.call-start = ((), (), s32[]{:S(2)}) async-start(), calls=%async_computation.3 | async-start | bytes 2097152 | tf_op jit(solution)/shard_map/psum | solution.py:39
  8.8 4.4 %copy-start.1 = (bf16[1536,512]{1,0:T(8,128)(2,1)S(1)}, bf16[1536,512]{1,0:T(8,128)(2,1)}, u32[]{:S(2)}) copy-start(bf16[1536,512]{1,0:T(8,128)(2,1)} %param.8) | copy-start | bytes 4718596
  14.5 120.0 %reduce-scatter.2.cloned.1.call-start = ((), (), s32[]{:S(2)}) async-start(), calls=%async_computation.2 | async-start | bytes 1769472 | tf_op jit(solution)/shard_map/reduce_scatter | solution.py:53
Sparse Core Ops, SparseCore 0:
  14.7 22.3 all-reduce.4
  72.4 62.0 reduce-scatter.1
where the time goes:
time: 145 us; the launch traced here: 144 us
  waiting for transfers between devices  59 us (41%)
  blocking collectives  46.3 us (32%)
  between operations  17.9 us (12%)
  matrix products  10.6 us (7%)
  other arithmetic  5.12 us (4%)
  local copies, waits for them, and re-layouts  5.01 us (3%)
    reduce_scatter x1, waiting for transfers between devices, body(): lax.psum_scatter(lax.dot_general(logit_grad, student_head, (((1,), (1,)),...  37.2 us
    psum x1, waiting for transfers between devices, body(): lax.psum((teacher_part, student_part), 'sect')  21.8 us
    psum x1, blocking collectives, body(): lax.psum((partial_sums[0], partial_sums[1], partial_sums[2]), 'vocab')  21.6 us
    all_to_all x1, blocking collectives, body(): lax.all_to_all(student_hidden, 'tok', split_axis=1, concat_axis=0, tiled=...  11.5 us
    all_gather x1, blocking collectives, body(): lax.all_gather(logit_grad, 'tok', axis=0, tiled=True)  7.05 us
    psum x1, blocking collectives, body(): loss = lax.psum(numerator, 'tok') / live_total  6.16 us
    dot_general x1, matrix products, body(): jnp.dot(teacher_hidden, teacher_head, preferred_element_type=jnp.float32)  4.34 us
    unnamed x8, local copies, waits for them, and re-layouts  3.86 us
  transfers between devices with their start and end apart: 2, of which 2 were waited for; matrix products, arithmetic and copies ran while one was open for 4% of the time, Pallas kernels for 0%

commit v1 on v0

--- a/solution.py
+++ b/solution.py
@@ -58,7 +58,7 @@
         scatter_dimension=0,
         tiled=True,
     ).astype(jnp.bfloat16)
-    loss = lax.psum(numerator, "tok") / live_total
+    loss = jnp.sum(lax.all_gather(numerator, "tok"), axis=0) / live_total
     return (loss, head_grad, hidden_grad)
 
 

time: 145 us -> 146 us (level)
  local copies, waits for them, and re-layouts: 5.01 us -> 7.06 us
    psum x1 -> x0, blocking collectives: 6.16 us -> none  [body(): loss = lax.psum(numerator, 'tok') / live_total]
    unnamed x0 -> x1, blocking collectives: none -> 6.13 us
    unnamed x8 -> x13, local copies, waits for them, and re-layouts: 3.86 us -> 5.9 us
where the time goes in v1:
time: 146 us; the launch traced here: 145 us
  waiting for transfers between devices  57.7 us (40%)
  blocking collectives  46.3 us (32%)
  between operations  17.9 us (12%)
  matrix products  10.6 us (7%)
  local copies, waits for them, and re-layouts  7.06 us (5%)
  other arithmetic  5.72 us (4%)
    reduce_scatter x1, waiting for transfers between devices, body(): lax.psum_scatter(lax.dot_general(logit_grad, student_head, (((1,), (1,)),...  36.5 us
    psum x1, blocking collectives, body(): lax.psum((partial_sums[0], partial_sums[1], partial_sums[2]), 'vocab')  21.6 us
    psum x1, waiting for transfers between devices, body(): lax.psum((teacher_part, student_part), 'sect')  21.1 us
    all_to_all x1, blocking collectives, body(): lax.all_to_all(student_hidden, 'tok', split_axis=1, concat_axis=0, tiled=...  11.5 us
    all_gather x1, blocking collectives, body(): lax.all_gather(logit_grad, 'tok', axis=0, tiled=True)  7.05 us
    unnamed x1, blocking collectives  6.13 us
    unnamed x13, local copies, waits for them, and re-layouts  5.9 us
    dot_general x1, matrix products, body(): jnp.dot(teacher_hidden, teacher_head, preferred_element_type=jnp.float32)  4.34 us
  transfers between devices with their start and end apart: 2, of which 2 were waited for; matrix products, arithmetic and copies ran while one was open for 4% of the time, Pallas kernels for 0%

profile of v1, /device:TPU:0, one launch (start us, length us, event | category | flops | bytes accessed | tf_op | source)
XLA Modules:
  0.0 145.4 jit_solution(12762695057096685967)
XLA Ops:
  7.2 0.0 all-reduce.6.cloned.1.call-start
  7.2 1.5 %copy-done = bf16[256,4096]{1,0:T(8,128)(2,1)S(1)} copy-done((bf16[256,4096]{1,0:T(8,128)(2,1)S(1)}, bf16[256,4096]{1,0:T(8,128)(2,1)}, u32[]{:S(2)}) %copy-start) | copy-done | bytes 2097176
  8.8 4.3 %fusion.3 = f32[256,512]{1,0:T(8,128)} fusion(bf16[256,4096]{1,0:T(8,128)(2,1)S(1)} %copy-done, bf16[4096,512]{1,0:T(8,128)(2,1)} %param.6), kind=kOutput, calls=%fused_computation.10 | convolution fusion | flops 1073741824 | bytes 6815744 | tf_op jit(solution)/shard_map/dot_general | solution.py:37
  13.1 1.4 fusion.4
  14.5 0.0 all-reduce.6.cloned.1.call-update
  14.5 0.0 reduce-scatter.2.cloned.1.call-start
  15.2 0.7 dynamic-slice
  15.9 21.1 %all-reduce.6.cloned.1.call-done = (f32[256,512]{1,0:T(8,128)}, f32[256,512]{1,0:T(8,128)}) async-done(((f32[256,512]{1,0:T(8,128)}, f32[256,512]{1,0:T(8,128)}), (f32[256,512]{1,0:T(8,128)}, f32[256,512]{1,0:T(8,128)})) %all-reduce.6.cloned.1.call-update) | async-done | bytes 1048592 | tf_op jit(solution)/shard_map/psum | solution.py:39
  37.1 1.5 %multiply_reduce_fusion = (f32[256]{0:T(256)S(1)}, f32[256]{0:T(256)S(1)}, f32[256]{0:T(256)S(1)}) fusion(f32[256,512]{1,0:T(8,128)} %get-tuple-element.20, f32[256,512]{1,0:T(8,128)} %get-tuple-element.21), kind=kLoop, calls=%fused_computation.3 | loop fusion | flops 916736 | bytes 1051648 | tf_op jit(solution)/shard_map/reduce_sum | solution.py:15
  38.6 21.6 %all-reduce.1 = (f32[256]{0:T(256)S(1)}, f32[256]{0:T(256)S(1)}, f32[256]{0:T(256)S(1)}) all-reduce(f32[256]{0:T(256)S(1)} %get-tuple-element.13, f32[256]{0:T(256)S(1)} %get-tuple-element.14, f32[256]{0:T(256)S(1)} %get-tuple-element.12), channel_id=1, replica_groups=mesh['sect'=2,'tok'=2,'vocab'=8] {'vocab'}, use_global_device_ids=true, to_apply=%region_7.0 | all-reduce | flops 768 | bytes 6144 | tf_op jit(solution)/shard_map/psum | solution.py:41
  60.2 0.6 select_reduce_fusion
  60.8 1.4 dynamic-update-slice
  62.2 6.1 %all-reduce.2 = (f32[2]{0:T(128)S(1)}, f32[]{:T(128)}) all-reduce(f32[2]{0:T(128)S(1)} %dynamic-update-slice, f32[]{:T(128)} %bitcast.3), channel_id=1, replica_groups=mesh['sect'=2,'tok'=2,'vocab'=8] {'tok'}, use_global_device_ids=true, to_apply=%add | all-reduce | flops 3 | bytes 24
  69.0 1.4 multiply_convert_fusion
  70.5 3.2 %fusion.5 = f32[256,1536]{1,0:T(8,128)} fusion(bf16[256,512]{1,0:T(8,128)(2,1)S(1)} %multiply_convert_fusion, bf16[1536,512]{1,0:T(8,128)(2,1)} %param.8), kind=kOutput, calls=%fused_computation.12 | convolution fusion | flops 402653184 | bytes 3407872 | tf_op jit(solution)/shard_map/dot_general | solution.py:54
  73.7 1.2 copy.10
  74.8 11.5 %all_to_all.19 = bf16[256,2,768]{0,2,1:T(8,128)(2,1)S(1)} all-to-all(bf16[256,2,768]{0,2,1:T(8,128)(2,1)} %bitcast.20), channel_id=1, replica_groups=mesh['sect'=2,'tok'=2,'vocab'=8] {'tok'}, dimensions={1} | all-to-all | bytes 1572864 | tf_op jit(solution)/shard_map/all_to_all | solution.py:45
  86.3 1.2 copy.11
  87.5 0.6 reduce_sum.55
  89.4 7.0 %all_gather.11 = bf16[512,512]{1,0:T(8,128)(2,1)S(1)} all-gather(bf16[256,512]{1,0:T(8,128)(2,1)S(1)} %multiply_convert_fusion), channel_id=1, replica_groups=mesh['sect'=2,'tok'=2,'vocab'=8] {'tok'}, dimensions={0}, use_global_device_ids=true | all-gather | bytes 786432 | tf_op jit(solution)/shard_map/all_gather | solution.py:48
  96.5 1.7 %fusion = bf16[768,512]{0,1:T(8,128)(2,1)S(1)} fusion(bf16[512,512]{1,0:T(8,128)(2,1)S(1)} %all_gather.11, bf16[512,768]{1,0:T(8,128)(2,1)} %bitcast.21), kind=kOutput, calls=%fused_computation.1 | convolution fusion | flops 403046400 | bytes 2097152 | tf_op jit(solution)/shard_map/dot_general | solution.py:46
  98.2 1.2 copy.12
  99.3 36.5 %reduce-scatter.2.cloned.1.call-done = f32[32,1536]{1,0:T(8,128)} async-done(((f32[256,1536]{1,0:T(8,128)}), f32[32,1536]{1,0:T(8,128)}) %reduce-scatter.2.cloned.1.call-update) | async-done | bytes 196624 | tf_op jit(solution)/shard_map/reduce_scatter | solution.py:53
  135.9 1.6 %convert_element_type.20 = bf16[32,1536]{1,0:T(8,128)(2,1)} convert(f32[32,1536]{1,0:T(8,128)} %reduce-scatter.2.cloned.1.call-done) | non-fusion elementwise | flops 49152 | bytes 294912 | tf_op jit(solution)/shard_map/convert_element_type | solution.py:60
  (10 shorter events, 0.0 us)
Async XLA Ops:
  7.2 1.6 %copy-start = (bf16[256,4096]{1,0:T(8,128)(2,1)S(1)}, bf16[256,4096]{1,0:T(8,128)(2,1)}, u32[]{:S(2)}) copy-start(bf16[256,4096]{1,0:T(8,128)(2,1)} %param.5) | copy-start | bytes 6291460
  7.2 5.9 %copy-start.2 = (bf16[256,1536]{1,0:T(8,128)(2,1)S(1)}, bf16[256,1536]{1,0:T(8,128)(2,1)}, u32[]{:S(2)}) copy-start(bf16[256,1536]{1,0:T(8,128)(2,1)} %param.7) | copy-start | bytes 2359300
  7.2 29.9 %all-reduce.6.cloned.1.call-start = ((), (), s32[]{:S(2)}) async-start(), calls=%async_computation.3 | async-start | bytes 2097152 | tf_op jit(solution)/shard_map/psum | solution.py:39
  8.8 4.4 %copy-start.1 = (bf16[1536,512]{1,0:T(8,128)(2,1)S(1)}, bf16[1536,512]{1,0:T(8,128)(2,1)}, u32[]{:S(2)}) copy-start(bf16[1536,512]{1,0:T(8,128)(2,1)} %param.8) | copy-start | bytes 4718596
  13.1 2.1 %copy-start.3 = (u32[32]{0:T(128)S(1)}, u32[32]{0:T(128)}, u32[]{:S(2)}) copy-start(u32[32]{0:T(128)} %constant.11) | copy-start | bytes 388
  14.5 121.3 %reduce-scatter.2.cloned.1.call-start = ((), (), s32[]{:S(2)}) async-start(), calls=%async_computation.2 | async-start | bytes 1769472 | tf_op jit(solution)/shard_map/reduce_scatter | solution.py:53
Sparse Core Ops, SparseCore 0:
  14.7 22.3 all-reduce.5
  73.8 62.0 reduce-scatter.1
